TPU v7x, 32 devices: a whole 2x2x4 slice. The times are simulated.
32 devices in a mesh: line: 2 (over x), track: 16 (over z, y, core).
Axes of the slice: x: 2, y: 2, z: 4, core: 2. Of those that a mesh axis runs over, the one named last changes fastest.
Arguments:
- radiance: bfloat16 [2, 64, 224, 1000], P('line', 'track'), may hold values from -40 to 40, as said below
Outputs:
- cleaned: bfloat16 [2, 64, 224, 1000], P('line', 'track')
- filter_matrix: float32 [224, 224], replicated
Inputs may be any that keep to these rules, and one draw needn't show every extreme that they name: `radiance`: every flightline, band and column carries a column offset, a column gain and pixel noise, so no column is constant along track.
All inputs are finite; a program needn't handle non-finite values.
Results may differ from a plain program's by a relative error of at most 0.0045.
Values may be sent and summed in bfloat16 or wider, within the bound.
A program may use at most 64 MiB of HBM per device.

v0:
```python
import jax
import jax.numpy as jnp
from jax import lax
from jax.sharding import PartitionSpec as P

NCOMP = 40
ITERS = 4


EPSILON = 1e-05
HIGHEST = lax.Precision.HIGHEST


def from_behind(block, axis, distance):
    devices = range(lax.axis_size(axis))
    route = [(i - distance, i) for i in devices if i - distance in devices]
    return lax.ppermute(block, axis, route)


def column_terms(first_total, second_total, total_rows):
    col_mean = first_total / total_rows
    col_spread = jnp.sqrt(second_total / total_rows - col_mean * col_mean + EPSILON)
    band_mean = jnp.mean(col_mean, axis=1)
    factor = jnp.mean(col_spread, axis=1)[:, None] / col_spread
    return (col_mean, factor, band_mean)


def pick_entry(vector, position, places):
    return jnp.sum(jnp.where(places == position, vector, 0.0))


def lower_factor(matrix):
    size = matrix.shape[0]
    places = jnp.arange(size)

    def one_column(column_id, factor):
        factor_row = lax.dynamic_slice_in_dim(factor, column_id, 1, 0)[0]
        column = lax.dynamic_slice_in_dim(matrix, column_id, 1, 1)[:, 0] - jnp.dot(
            factor, factor_row, precision=HIGHEST
        )
        pivot = jnp.sqrt(pick_entry(column, column_id, places))
        entries = jnp.where(places == column_id, pivot, column / pivot)
        entries = jnp.where(places >= column_id, entries, 0.0)
        return jnp.where(places[None, :] == column_id, entries[:, None], factor)

    return lax.fori_loop(0, size, one_column, jnp.zeros_like(matrix))


def lower_solve(factor, right_side):
    size = factor.shape[0]
    places = jnp.arange(size)

    def one_row(row_id, solved):
        factor_row = lax.dynamic_slice_in_dim(factor, row_id, 1, 0)[0]
        target = lax.dynamic_slice_in_dim(right_side, row_id, 1, 0)[0]
        pivot = pick_entry(factor_row, row_id, places)
        entries = (target - jnp.dot(factor_row, solved, precision=HIGHEST)) / pivot
        return lax.dynamic_update_slice_in_dim(solved, entries[None], row_id, 0)

    return lax.fori_loop(0, size, one_row, jnp.zeros_like(right_side))


def upper_solve(factor, right_side):
    flipped = factor.T[::-1, ::-1]
    return lower_solve(flipped, right_side[::-1])[::-1]


def mnf_filter(signal_gram, noise_gram, kept):
    noise_factor = lower_factor(noise_gram)
    half_solved = lower_solve(noise_factor, signal_gram)
    whitened = lower_solve(noise_factor, half_solved.T)
    whitened = 0.5 * (whitened + whitened.T)
    subspace = jnp.eye(whitened.shape[0], kept, dtype=jnp.float32)
    for iteration in range(ITERS):
        mapped = jnp.dot(whitened, subspace, precision=HIGHEST)
        inner_gram = jnp.dot(mapped.T, mapped, precision=HIGHEST)
        inner_factor = lower_factor(inner_gram)
        subspace = lower_solve(inner_factor, mapped.T).T
    forward_map = upper_solve(noise_factor, subspace)
    backward_map = jnp.dot(noise_factor, subspace, precision=HIGHEST)
    return jnp.dot(forward_map, backward_map.T, precision=HIGHEST)


def body(radiance):
    local_block = radiance[0]
    row_count = local_block.shape[0]
    column_count = local_block.shape[2]
    track_count = lax.axis_size("track")
    line_count = lax.axis_size("line")
    total_rows = row_count * track_count
    values = local_block.astype(jnp.float32)
    first_sum = jnp.sum(values, axis=0)
    second_sum = jnp.sum(values * values, axis=0)
    first_total, second_total = lax.psum((first_sum, second_sum), "track")
    col_mean, factor, band_mean = column_terms(first_total, second_total, total_rows)
    centred = ((values - col_mean) * factor).astype(jnp.bfloat16)
    following = from_behind(centred[:1], "track", -1)
    rows_ahead = jnp.concatenate([centred[1:], following], axis=0)
    keep_last = lax.axis_index("track") < track_count - 1
    row_index = jnp.arange(row_count)
    row_keep = jnp.where((row_index < row_count - 1) | keep_last, 1.0, 0.0).astype(jnp.float32)
    differences = (
        (rows_ahead.astype(jnp.float32) - centred.astype(jnp.float32)) * row_keep[:, None, None]
    ).astype(jnp.bfloat16)
    signal_part = jnp.einsum("rbc,rdc->bd", centred, centred, preferred_element_type=jnp.float32)
    noise_part = jnp.einsum(
        "rbc,rdc->bd", differences, differences, preferred_element_type=jnp.float32
    )
    signal_total, noise_total = lax.psum((signal_part, noise_part), ("line", "track"))
    signal_gram = signal_total / (line_count * total_rows * column_count)
    noise_gram = noise_total / (2 * line_count * (total_rows - 1) * column_count)
    filter_matrix = mnf_filter(signal_gram, noise_gram, NCOMP)
    narrow = filter_matrix.astype(jnp.bfloat16)
    mixed = jnp.einsum("ab,rac->rbc", narrow, centred, preferred_element_type=jnp.float32)
    cleaned = (band_mean[:, None] + mixed).astype(jnp.bfloat16)
    return (cleaned[None], filter_matrix)


def solution(mesh):
    in_specs = (P("line", "track", None, None),)
    out_specs = (P("line", "track", None, None), P())
    return jax.shard_map(body, mesh=mesh, in_specs=in_specs, out_specs=out_specs, check_vma=False)
```

profile of v0, /device:TPU:0, one launch (start us, length us, event | category | flops | bytes accessed | tf_op | source)
XLA Modules:
  0.0 2185.9 jit_solution(16834112207716151684)
XLA Ops:
  7.2 3.0 convert_reduce_fusion
  10.2 1.3 fusion.71
  11.6 100.6 %all-reduce.7.cloned.1.call-done = (f32[224,1000]{1,0:T(8,128)}, f32[224,1000]{1,0:T(8,128)}) async-done(((f32[224,1000]{1,0:T(8,128)}, f32[224,1000]{1,0:T(8,128)}), (f32[224,1000]{1,0:T(8,128)}, f32[224,1000]{1,0:T(8,128)})) %all-reduce.7.cloned.1.call-update) | async-done | bytes 1792016 | tf_op jit(solution)/shard_map/psum | solution.py:94
  112.1 2.2 fusion.85
  114.9 1.0 copy-done.1
  116.5 1.3 collective-permute-start
  118.0 1.4 convolution_bitcast_fusion.5
  119.4 0.9 collective-permute-done
  120.2 2.0 fusion.78
  122.3 132.4 %all-reduce.5.cloned.1.call-done = (f32[224,224]{1,0:T(8,128)}, f32[224,224]{1,0:T(8,128)}) async-done(((f32[224,224]{1,0:T(8,128)}, f32[224,224]{1,0:T(8,128)}), (f32[224,224]{1,0:T(8,128)}, f32[224,224]{1,0:T(8,128)})) %all-reduce.5.cloned.1.call-update) | async-done | bytes 401424 | tf_op jit(solution)/shard_map/psum | solution.py:109
  254.7 1.1 broadcast_multiply_fusion.1
  255.9 401.2 %while.180 = (s32[]{:T(128)}, f32[224,224]{1,0:T(8,128)S(1)}, f32[224,224]{0,1:T(8,128)S(1)}, s32[]{:T(128)}, s32[]{:T(128)}) while((s32[]{:T(128)}, f32[224,224]{1,0:T(8,128)S(1)}, f32[224,224]{0,1:T(8,128)S(1)}, s32[]{:T(128)}, s32[]{:T(128)}) %tuple.370), condition=%wide.region_9.10_spmd.clone.clone, body=%wide.region_7.0_spmd.clone.clone.sunk | while | flops 754882 | bytes 1041836 | solution.py:46
  657.1 346.7 %while.173 = (s32[]{:T(128)}, f32[224,224]{1,0:T(8,128)S(1)}, f32[224,224]{1,0:T(8,128)S(1)}, f32[224,224]{1,0:T(8,128)S(1)}, s32[]{:T(128)}, /*index=5*/s32[]{:T(128)}) while((s32[]{:T(128)}, f32[224,224]{1,0:T(8,128)S(1)}, f32[224,224]{1,0:T(8,128)S(1)}, f32[224,224]{1,0:T(8,128)S(1)}, s32[]{:T(128)}, ...), condition=%wide.region_13.14_spmd.clone, body=%wide.region_11.13_spmd.clone.sunk | while | flops 603233 | bytes 211545 | solution.py:60
  1004.0 346.7 %while.174 = (s32[]{:T(128)}, f32[224,224]{1,0:T(8,128)S(1)}, f32[224,224]{1,0:T(8,128)S(1)}, f32[224,224]{1,0:T(8,128)S(1)}, s32[]{:T(128)}, /*index=5*/s32[]{:T(128)}) while((s32[]{:T(128)}, f32[224,224]{1,0:T(8,128)S(1)}, f32[224,224]{1,0:T(8,128)S(1)}, f32[224,224]{1,0:T(8,128)S(1)}, s32[]{:T(128)}, ...), condition=%wide.region_16.17_spmd.clone, body=%wide.region_14.16_spmd.clone.sunk | while | flops 603233 | bytes 211545 | solution.py:60
  1351.3 62.4 %while.181 = (s32[]{:T(128)}, f32[40,40]{1,0:T(8,128)S(1)}, f32[40,40]{0,1:T(8,128)S(1)}, s32[]{:T(128)}, s32[]{:T(128)}) while((s32[]{:T(128)}, f32[40,40]{1,0:T(8,128)S(1)}, f32[40,40]{0,1:T(8,128)S(1)}, s32[]{:T(128)}, s32[]{:T(128)}) %tuple.379), condition=%wide.region_19.20_spmd.clone.clone, body=%wide.region_17.19_spmd.clone.clone.sunk | while | flops 24402 | bytes 49456 | solution.py:46
  1413.8 58.8 %while.175 = (s32[]{:T(128)}, f32[40,224]{1,0:T(8,128)S(1)}, f32[40,224]{1,0:T(8,128)S(1)}, f32[40,40]{1,0:T(8,128)S(1)}, s32[]{:T(128)}, /*index=5*/s32[]{:T(128)}) while((s32[]{:T(128)}, f32[40,224]{1,0:T(8,128)S(1)}, f32[40,224]{1,0:T(8,128)S(1)}, f32[40,40]{1,0:T(8,128)S(1)}, s32[]{:T(128)}, /*index=5*/s32[]{:T(128)}) %tuple.416), condition=%wide.region_22.23_spmd.clone, body=%wide.region_20.22_spmd.clone.sunk | while | flops 108089 | bytes 49913 | solution.py:60
  1473.0 62.4 %while.182 = (s32[]{:T(128)}, f32[40,40]{1,0:T(8,128)S(1)}, f32[40,40]{0,1:T(8,128)S(1)}, s32[]{:T(128)}, s32[]{:T(128)}) while((s32[]{:T(128)}, f32[40,40]{1,0:T(8,128)S(1)}, f32[40,40]{0,1:T(8,128)S(1)}, s32[]{:T(128)}, s32[]{:T(128)}) %tuple.385), condition=%wide.region_25.26_spmd.clone.clone, body=%wide.region_23.25_spmd.clone.clone.sunk | while | flops 24402 | bytes 49456 | solution.py:46
  1535.5 58.8 %while.176 = (s32[]{:T(128)}, f32[40,224]{1,0:T(8,128)S(1)}, f32[40,224]{1,0:T(8,128)S(1)}, f32[40,40]{1,0:T(8,128)S(1)}, s32[]{:T(128)}, /*index=5*/s32[]{:T(128)}) while((s32[]{:T(128)}, f32[40,224]{1,0:T(8,128)S(1)}, f32[40,224]{1,0:T(8,128)S(1)}, f32[40,40]{1,0:T(8,128)S(1)}, s32[]{:T(128)}, /*index=5*/s32[]{:T(128)}) %tuple.414), condition=%wide.region_28.29_spmd.clone, body=%wide.region_26.28_spmd.clone.sunk | while | flops 108089 | bytes 49913 | solution.py:60
  1594.8 62.4 %while.183 = (s32[]{:T(128)}, f32[40,40]{1,0:T(8,128)S(1)}, f32[40,40]{0,1:T(8,128)S(1)}, s32[]{:T(128)}, s32[]{:T(128)}) while((s32[]{:T(128)}, f32[40,40]{1,0:T(8,128)S(1)}, f32[40,40]{0,1:T(8,128)S(1)}, s32[]{:T(128)}, s32[]{:T(128)}) %tuple.391), condition=%wide.region_31.32_spmd.clone.clone, body=%wide.region_29.31_spmd.clone.clone.sunk | while | flops 24402 | bytes 49456 | solution.py:46
  1657.2 58.8 %while.177 = (s32[]{:T(128)}, f32[40,224]{1,0:T(8,128)S(1)}, f32[40,224]{1,0:T(8,128)S(1)}, f32[40,40]{1,0:T(8,128)S(1)}, s32[]{:T(128)}, /*index=5*/s32[]{:T(128)}) while((s32[]{:T(128)}, f32[40,224]{1,0:T(8,128)S(1)}, f32[40,224]{1,0:T(8,128)S(1)}, f32[40,40]{1,0:T(8,128)S(1)}, s32[]{:T(128)}, /*index=5*/s32[]{:T(128)}) %tuple.415), condition=%wide.region_34.35_spmd.clone, body=%wide.region_32.34_spmd.clone.sunk | while | flops 108089 | bytes 49913 | solution.py:60
  1716.4 62.4 %while.184 = (s32[]{:T(128)}, f32[40,40]{1,0:T(8,128)S(1)}, f32[40,40]{0,1:T(8,128)S(1)}, s32[]{:T(128)}, s32[]{:T(128)}) while((s32[]{:T(128)}, f32[40,40]{1,0:T(8,128)S(1)}, f32[40,40]{0,1:T(8,128)S(1)}, s32[]{:T(128)}, s32[]{:T(128)}) %tuple.397), condition=%wide.region_37.38_spmd.clone.clone, body=%wide.region_35.37_spmd.clone.clone.sunk | while | flops 24402 | bytes 49456 | solution.py:46
  1778.9 58.8 %while.178 = (s32[]{:T(128)}, f32[40,224]{1,0:T(8,128)S(1)}, f32[40,224]{1,0:T(8,128)S(1)}, f32[40,40]{1,0:T(8,128)S(1)}, s32[]{:T(128)}, /*index=5*/s32[]{:T(128)}) while((s32[]{:T(128)}, f32[40,224]{1,0:T(8,128)S(1)}, f32[40,224]{1,0:T(8,128)S(1)}, f32[40,40]{1,0:T(8,128)S(1)}, s32[]{:T(128)}, /*index=5*/s32[]{:T(128)}) %tuple.413), condition=%wide.region_40.41_spmd.clone, body=%wide.region_38.40_spmd.clone.sunk | while | flops 108089 | bytes 49913 | solution.py:60
  1839.4 336.9 %while.179 = (s32[]{:T(128)}, f32[224,40]{1,0:T(8,128)S(1)}, f32[224,40]{1,0:T(8,128)S(1)}, f32[224,224]{1,0:T(8,128)S(1)}, s32[]{:T(128)}, /*index=5*/s32[]{:T(128)}) while((s32[]{:T(128)}, f32[224,40]{1,0:T(8,128)S(1)}, f32[224,40]{1,0:T(8,128)S(1)}, f32[224,224]{1,0:T(8,128)S(1)}, s32[]{:T(128)}, /*index=5*/s32[]{:T(128)}) %tuple.403), condition=%wide.region_43.44_spmd.clone, body=%wide.region_41.43_spmd.clone.sunk | while | flops 108273 | bytes 121013 | solution.py:60
  1841.5 0.8 fusion.191
  1844.5 0.8 fusion.191
  1846.0 0.8 fusion.191
  1847.5 0.8 fusion.191
  1849.0 0.8 fusion.191
  1852.1 0.8 fusion.191
  1855.1 0.8 fusion.191
  1858.1 0.8 fusion.191
  2177.0 2.1 fusion.77
  (6348 shorter events, 1607.1 us)
Async XLA Ops:
  7.2 3.0 copy-start
  7.2 105.0 %all-reduce.7.cloned.1.call-start = ((), (), s32[]{:S(2)}) async-start(), calls=%async_computation.1 | async-start | bytes 3670016 | tf_op jit(solution)/shard_map/psum | solution.py:94
  11.5 243.1 %all-reduce.5.cloned.1.call-start = ((), (), s32[]{:S(2)}) async-start(), calls=%async_computation | async-start | bytes 917504 | tf_op jit(solution)/shard_map/psum | solution.py:109
  112.1 2.3 copy-start.2
  112.1 2.3 copy-start.3
  114.4 1.5 copy-start.1
  116.5 3.7 collective-permute-start
  2177.0 2.1 copy-start.4
Sparse Core Ops, SparseCore 0:
  12.1 99.9 all-reduce.6
  122.4 132.2 all-reduce.4
where the time goes:
time: 2200 us; the launch traced here: 2190 us
  other arithmetic  1100 us (50%)
  matrix products  467 us (21%)
  loops' own time  309 us (14%)
  waiting for transfers between devices  234 us (11%)
  local copies, waits for them, and re-layouts  62 us (3%)
    reduce_sum x1056, other arithmetic, pick_entry(): return jnp.sum(jnp.where(places == position, vector, 0.0))  636 us
    div x608, other arithmetic, one_row(): entries = (target - jnp.dot(factor_row, solved, precision=HIGHEST)) / pivot  409 us
    dot_general x832, matrix products, one_row(): entries = (target - jnp.dot(factor_row, solved, precision=HIGHEST)) / pivot  285 us
    another operation x5, loops' own time, lower_factor(): return lax.fori_loop(0, size, one_column, jnp.zeros_like(matrix))  281 us
    dot_general x384, matrix products, one_column(): jnp.dot(factor, factor_row, precision=HIGHEST)  174 us
    psum x1, waiting for transfers between devices, body(): lax.psum((signal_part, noise_part), ('line', 'track'))  132 us
    psum x1, waiting for transfers between devices, body(): first_total, second_total = lax.psum((first_sum, second_sum), 'track')  101 us

commit v1 on v0

v1 whole, which is shorter than its diff:
```python
import functools

import jax
import jax.numpy as jnp
from jax import lax
from jax.experimental import pallas as pl
from jax.experimental.pallas import tpu as pltpu
from jax.sharding import PartitionSpec as P

NCOMP = 40
ITERS = 4


EPSILON = 1e-05
HIGHEST = lax.Precision.HIGHEST


def from_behind(block, axis, distance):
    devices = range(lax.axis_size(axis))
    route = [(i - distance, i) for i in devices if i - distance in devices]
    return lax.ppermute(block, axis, route)


def column_terms(first_total, second_total, total_rows):
    col_mean = first_total / total_rows
    col_spread = jnp.sqrt(second_total / total_rows - col_mean * col_mean + EPSILON)
    band_mean = jnp.mean(col_mean, axis=1)
    factor = jnp.mean(col_spread, axis=1)[:, None] / col_spread
    return (col_mean, factor, band_mean)


PANEL = 32
GROUP = 8


def contract(left, right, left_axis, right_axis):
    return lax.dot_general(
        left, right, (((left_axis,), (right_axis,)), ((), ())),
        precision=HIGHEST, preferred_element_type=jnp.float32,
    )


def eliminate(panel, offset):
    size = panel.shape[0]
    row_ids = lax.broadcasted_iota(jnp.int32, (size, 128), 0)
    repeats = panel.shape[1] // 128
    tiles = [panel[:, t * 128:(t + 1) * 128] for t in range(repeats)]
    home, shift = divmod(offset, 128)
    scales = jnp.zeros((size, 128), jnp.float32)
    for start in range(0, size, GROUP):
        lanes = range(start, min(start + GROUP, size))
        columns = {}
        for k in lanes:
            tile, lane = divmod(offset + k, 128)
            columns[k] = jnp.broadcast_to(tiles[tile][:, lane:lane + 1], (size, 128))
        for k in lanes:
            pivot_row = jnp.broadcast_to(columns[k][k:k + 1], (size, 128))
            scales = jnp.where(row_ids == k, pivot_row, scales)
            step = jnp.where(row_ids > k, columns[k] * (1.0 / pivot_row), 0.0)
            for later in lanes:
                if later > k:
                    columns[later] = columns[later] - step * columns[later][k:k + 1]
            tiles = [tile - step * tile[k:k + 1] for tile in tiles]
    scales = 1.0 / jnp.sqrt(scales)
    return jnp.concatenate([tile * scales for tile in tiles], axis=1)


def mnf_kernel(signal_scale, noise_scale, kept, signal_ref, noise_ref, filter_ref, work):
    size = signal_ref.shape[0]
    wide = work.shape[1] // 3
    work[...] = jnp.zeros_like(work)
    work[:, :size] = noise_ref[...] * noise_scale
    ids = lax.broadcasted_iota(jnp.int32, (size, size), 0)
    work[:, wide:wide + size] = jnp.where(
        ids == lax.broadcasted_iota(jnp.int32, (size, size), 1), 1.0, 0.0
    )
    work[:, 2 * wide:2 * wide + size] = signal_ref[...] * signal_scale
    for start in range(0, size, PANEL):
        end = min(start + PANEL, size)
        rows = eliminate(work[start:end, :], start)
        work[start:end, :] = rows
        if end < size:
            step = contract(rows[:, end:size], rows, 0, 0)
            work[end:, :] = work[end:, :] - step
    upper = work[:, :wide]
    upper = jnp.where(
        lax.broadcasted_iota(jnp.int32, (size, wide), 1)
        >= lax.broadcasted_iota(jnp.int32, (size, wide), 0),
        upper, 0.0,
    )
    inverse = work[:, wide:2 * wide]
    half_solved = work[:, 2 * wide:]
    margin = jnp.zeros((wide - size, wide), jnp.float32)
    inner = contract(
        jnp.concatenate([half_solved, margin], axis=0),
        jnp.concatenate([inverse, margin], axis=0), 1, 1,
    )
    whitened = 0.5 * (inner + inner.T)
    mapped = whitened[:kept]
    for iteration in range(ITERS):
        if iteration:
            mapped = contract(mapped, whitened, 1, 0)
        gram = contract(mapped, mapped, 1, 1)
        gram = jnp.concatenate([gram, jnp.zeros((kept, 128 - kept), jnp.float32)], axis=1)
        mapped = eliminate(jnp.concatenate([gram, mapped], axis=1), 0)[:, 128:]
    subspace = mapped[:, :size]
    forward = contract(subspace, inverse, 1, 0)
    backward = contract(subspace, upper, 1, 0)
    filter_ref[...] = contract(forward, backward, 0, 0)[:size, :size]


def mnf_filter(signal_total, noise_total, signal_count, noise_count, kept):
    size = signal_total.shape[0]
    wide = -(-size // 128) * 128
    kernel = functools.partial(mnf_kernel, 1.0 / signal_count, 1.0 / noise_count, kept)
    return pl.pallas_call(
        kernel,
        out_shape=jax.ShapeDtypeStruct((size, size), jnp.float32),
        in_specs=[pl.BlockSpec(memory_space=pltpu.VMEM)] * 2,
        out_specs=pl.BlockSpec(memory_space=pltpu.VMEM),
        scratch_shapes=[pltpu.VMEM((size, 3 * wide), jnp.float32)],
        name="mnf_filter",
    )(signal_total, noise_total)


def body(radiance):
    local_block = radiance[0]
    row_count = local_block.shape[0]
    column_count = local_block.shape[2]
    track_count = lax.axis_size("track")
    line_count = lax.axis_size("line")
    total_rows = row_count * track_count
    values = local_block.astype(jnp.float32)
    first_sum = jnp.sum(values, axis=0)
    second_sum = jnp.sum(values * values, axis=0)
    first_total, second_total = lax.psum((first_sum, second_sum), "track")
    col_mean, factor, band_mean = column_terms(first_total, second_total, total_rows)
    centred = ((values - col_mean) * factor).astype(jnp.bfloat16)
    following = from_behind(centred[:1], "track", -1)
    rows_ahead = jnp.concatenate([centred[1:], following], axis=0)
    keep_last = lax.axis_index("track") < track_count - 1
    row_index = jnp.arange(row_count)
    row_keep = jnp.where((row_index < row_count - 1) | keep_last, 1.0, 0.0).astype(jnp.float32)
    differences = (
        (rows_ahead.astype(jnp.float32) - centred.astype(jnp.float32)) * row_keep[:, None, None]
    ).astype(jnp.bfloat16)
    signal_part = jnp.einsum("rbc,rdc->bd", centred, centred, preferred_element_type=jnp.float32)
    noise_part = jnp.einsum(
        "rbc,rdc->bd", differences, differences, preferred_element_type=jnp.float32
    )
    signal_total, noise_total = lax.psum((signal_part, noise_part), ("line", "track"))
    signal_count = line_count * total_rows * column_count
    noise_count = 2 * line_count * (total_rows - 1) * column_count
    filter_matrix = mnf_filter(signal_total, noise_total, signal_count, noise_count, NCOMP)
    narrow = filter_matrix.astype(jnp.bfloat16)
    mixed = jnp.einsum("ab,rac->rbc", narrow, centred, preferred_element_type=jnp.float32)
    cleaned = (band_mean[:, None] + mixed).astype(jnp.bfloat16)
    return (cleaned[None], filter_matrix)


def solution(mesh):
    in_specs = (P("line", "track", None, None),)
    out_specs = (P("line", "track", None, None), P())
    return jax.shard_map(body, mesh=mesh, in_specs=in_specs, out_specs=out_specs, check_vma=False)
```

time: 2200 us -> 282 us (0.13)
  other arithmetic: 1100 us -> 7.56 us
  matrix products: 467 us -> 6.36 us
  loops' own time: 309 us -> 0 us
  local copies, waits for them, and re-layouts: 62 us -> 1.18 us
    reduce_sum x1056 -> x0, other arithmetic: 636 us -> none  [pick_entry(): return jnp.sum(jnp.where(places == position, vector, 0.0))]
    dot_general x1226 -> x0, matrix products: 462 us -> none  [the longest x832 285 us: one_row(): entries = (target - jnp.dot(factor_row, solved, precision=HIGHEST)) / pivot]
    div x609 -> x0, other arithmetic: 410 us -> none  [the longest x608 409 us: one_row(): entries = (target - jnp.dot(factor_row, solved, precision=HIGHEST)) / pivot]
    another operation x12 -> x0, loops' own time: 309 us -> none  [the longest x5 281 us: lower_factor(): return lax.fori_loop(0, size, one_column, jnp.zeros_like(matrix))]
    select_n x768 -> x0, other arithmetic: 37.8 us -> none  [the longest x384 35.4 us: one_column(): return jnp.where(places[None, :] == column_id, entries[:, None], factor)]
    dynamic_update_slice x832 -> x0, local copies, waits for them, and re-layouts: 35.7 us -> none  [one_row(): return lax.dynamic_update_slice_in_dim(solved, entries[None], row_id, 0)]
    dynamic_slice x1056 -> x0, local copies, waits for them, and re-layouts: 23.1 us -> none  [the longest x224 15.3 us: one_column(): lax.dynamic_slice_in_dim(matrix, column_id, 1, 1)[:, 0]]
where the time goes in v1:
time: 282 us; the launch traced here: 281 us
  waiting for transfers between devices  234 us (83%)
  Pallas kernels  16.8 us (6%)
  between operations  14.1 us (5%)
  other arithmetic  7.56 us (3%)
  matrix products  6.36 us (2%)
    psum x1, waiting for transfers between devices, body(): lax.psum((signal_part, noise_part), ('line', 'track'))  132 us
    psum x1, waiting for transfers between devices, body(): first_total, second_total = lax.psum((first_sum, second_sum), 'track')  101 us
    pallas_call x1, Pallas kernels, mnf_filter(): pl.pallas_call(kernel, out_shape=jax.ShapeDtypeStruct((size, size), jnp.f...  16.8 us
  transfers between devices with their start and end apart: 3, of which 3 were waited for; matrix products, arithmetic and copies ran while one was open for 1% of the time, Pallas kernels for 0%

profile of v1, /device:TPU:0, one launch (start us, length us, event | category | flops | bytes accessed | tf_op | source)
XLA Modules:
  0.0 281.2 jit_solution(12011226877473572837)
XLA Ops:
  7.2 0.0 copy-start
  7.2 0.0 all-reduce.7.cloned.1.call-start
  7.2 3.0 %fusion.4 = f32[224,1000]{1,0:T(8,128)} fusion(bf16[1,4,224,1000]{3,2,1,0:T(8,128)(2,1)} %param.1), kind=kLoop, calls=%fused_computation.6 | loop fusion | flops 2464000 | bytes 2688000 | tf_op jit(solution)/shard_map/reduce_sum | solution.py:135
  10.3 0.0 copy-done
  10.3 1.3 convert_reduce_fusion
  11.5 0.0 all-reduce.7.cloned.1.call-update
  11.5 0.0 all-reduce.5.cloned.1.call-start
  11.6 100.6 %all-reduce.7.cloned.1.call-done = (f32[224,1000]{1,0:T(8,128)}, f32[224,1000]{1,0:T(8,128)}) async-done(((f32[224,1000]{1,0:T(8,128)}, f32[224,1000]{1,0:T(8,128)}), (f32[224,1000]{1,0:T(8,128)}, f32[224,1000]{1,0:T(8,128)})) %all-reduce.7.cloned.1.call-update) | async-done | bytes 1792016 | tf_op jit(solution)/shard_map/psum | solution.py:136
  112.1 0.0 copy-start.2
  112.1 0.0 copy-start.3
  112.1 2.2 fusion.16
  114.4 0.0 copy-start.1
  114.4 0.0 copy-done.2
  114.4 0.0 copy-done.3
  114.4 0.4 broadcast_divide_fusion
  114.9 1.0 copy-done.1
  115.9 0.6 fusion.3
  116.5 1.5 collective-permute-start
  118.0 0.1 slice.8
  118.1 1.4 convolution_bitcast_fusion
  119.5 0.7 collective-permute-done
  120.2 2.0 fusion.11
  122.2 0.0 all-reduce.5.cloned.1.call-update
  122.3 132.3 %all-reduce.5.cloned.1.call-done = (f32[224,224]{1,0:T(8,128)}, f32[224,224]{1,0:T(8,128)}) async-done(((f32[224,224]{1,0:T(8,128)}, f32[224,224]{1,0:T(8,128)}), (f32[224,224]{1,0:T(8,128)}, f32[224,224]{1,0:T(8,128)})) %all-reduce.5.cloned.1.call-update) | async-done | bytes 401424 | tf_op jit(solution)/shard_map/psum | solution.py:151
  254.6 16.8 %mnf_filter.1 = f32[224,224]{1,0:T(8,128)} custom-call(f32[224,224]{1,0:T(8,128)} %get-tuple-element.4.signal_ref, f32[224,224]{1,0:T(8,128)} %get-tuple-element.5.noise_ref), custom_call_target="tpu_custom_call" | custom-call | tf_op jit(solution)/shard_map/mnf_filter/pallas_call | solution.py:116
  271.3 3.0 %fusion.10 = bf16[1,4,224,1000]{3,2,1,0:T(8,128)(2,1)} fusion(bf16[4,224,1000]{2,1,0:T(8,128)(2,1)S(1)} %fusion.3, f32[224]{0:T(256)S(1)} %broadcast_multiply_fusion.2, f32[224,224]{1,0:T(8,128)} %mnf_filter.1), kind=kOutput, calls=%fused_computation.14 | convolution fusion | flops 403250176 | bytes 3785600 | tf_op jit(solution)/shard_map/ab,rac->rbc/dot_general | solution.py:156
  (4 shorter events, 0.0 us)
Async XLA Ops:
  7.2 3.1 %copy-start = (bf16[1,4,224,1000]{3,2,1,0:T(8,128)(2,1)S(1)}, bf16[1,4,224,1000]{3,2,1,0:T(8,128)(2,1)}, u32[]{:S(2)}) copy-start(bf16[1,4,224,1000]{3,2,1,0:T(8,128)(2,1)} %param.1) | copy-start | bytes 5376004
  7.2 105.0 %all-reduce.7.cloned.1.call-start = ((), (), s32[]{:S(2)}) async-start(), calls=%async_computation.1 | async-start | bytes 3670016 | tf_op jit(solution)/shard_map/psum | solution.py:136
  11.5 243.0 %all-reduce.5.cloned.1.call-start = ((), (), s32[]{:S(2)}) async-start(), calls=%async_computation | async-start | bytes 917504 | tf_op jit(solution)/shard_map/psum | solution.py:151
  112.1 2.3 copy-start.2
  112.1 2.3 copy-start.3
  114.4 1.5 copy-start.1
  116.5 3.7 %collective-permute-start = (bf16[1,224,1000]{2,1,0:T(8,128)(2,1)S(1)}, bf16[1,224,1000]{2,1,0:T(8,128)(2,1)S(1)}, u32[]{:S(2)}, u32[]{:S(2)}) collective-permute-start(bf16[1,224,1000]{2,1,0:T(8,128)(2,1)S(1)} %slice.9), channel_id=1, source_target_pairs={{1,0},{2,1},{3,2},{4,3},{5,4},{6,5},{7,6},{8,7},{9,8},{10,9},{11,1... | collective-permute-start | bytes 1344008 | tf_op jit(solution)/shard_map/ppermute | solution.py:21
Sparse Core Ops, SparseCore 0:
  12.1 99.9 all-reduce.6
  122.4 132.1 all-reduce.4

commit v2 on v1

--- a/solution.py
+++ b/solution.py
@@ -65,16 +65,20 @@
     return jnp.concatenate([tile * scales for tile in tiles], axis=1)
 
 
-def mnf_kernel(signal_scale, noise_scale, kept, signal_ref, noise_ref, filter_ref, work):
-    size = signal_ref.shape[0]
-    wide = work.shape[1] // 3
-    work[...] = jnp.zeros_like(work)
-    work[:, :size] = noise_ref[...] * noise_scale
-    ids = lax.broadcasted_iota(jnp.int32, (size, size), 0)
-    work[:, wide:wide + size] = jnp.where(
-        ids == lax.broadcasted_iota(jnp.int32, (size, size), 1), 1.0, 0.0
-    )
-    work[:, 2 * wide:2 * wide + size] = signal_ref[...] * signal_scale
+def mnf_kernel(signal_scale, noise_scale, kept, packed_ref, filter_ref, work):
+    size = filter_ref.shape[0]
+    wide = packed_ref.shape[0]
+    packed = packed_ref[...]
+    row_ids = lax.broadcasted_iota(jnp.int32, (wide, wide), 0)
+    column_ids = lax.broadcasted_iota(jnp.int32, (wide, wide), 1)
+    below = jnp.where((row_ids > column_ids) & (row_ids < size), packed, 0.0)
+    above = jnp.where(row_ids < column_ids, packed, 0.0)
+    diagonal = row_ids == column_ids
+    noise = below + below.T + jnp.where(diagonal, packed, 0.0)
+    signal = above + above.T + jnp.where(diagonal, packed[size:size + 1], 0.0)
+    work[:, :wide] = noise[:size] * noise_scale
+    work[:, wide:2 * wide] = jnp.where(diagonal, 1.0, 0.0)[:size]
+    work[:, 2 * wide:] = signal[:size] * signal_scale
     for start in range(0, size, PANEL):
         end = min(start + PANEL, size)
         rows = eliminate(work[start:end, :], start)
@@ -109,18 +113,183 @@
     filter_ref[...] = contract(forward, backward, 0, 0)[:size, :size]
 
 
-def mnf_filter(signal_total, noise_total, signal_count, noise_count, kept):
-    size = signal_total.shape[0]
-    wide = -(-size // 128) * 128
-    kernel = functools.partial(mnf_kernel, 1.0 / signal_count, 1.0 / noise_count, kept)
+def mnf_filter(packed, size, signal_count, noise_count, kept):
+    wide = packed.shape[0]
     return pl.pallas_call(
-        kernel,
+        functools.partial(mnf_kernel, 1.0 / signal_count, 1.0 / noise_count, kept),
         out_shape=jax.ShapeDtypeStruct((size, size), jnp.float32),
-        in_specs=[pl.BlockSpec(memory_space=pltpu.VMEM)] * 2,
+        in_specs=[pl.BlockSpec(memory_space=pltpu.VMEM)],
         out_specs=pl.BlockSpec(memory_space=pltpu.VMEM),
         scratch_shapes=[pltpu.VMEM((size, 3 * wide), jnp.float32)],
         name="mnf_filter",
-    )(signal_total, noise_total)
+    )(packed)
+
+
+def track_place(track):
+    return (lax.axis_index("line"), track)
+
+
+def stats_kernel(tracks, x_ref, out_ref, paired, mine, slots, gathered, other, send, recv):
+    chips = tracks // 2
+    half = x_ref.shape[1] // 2
+    width = x_ref.shape[2] // chips
+    track = lax.axis_index("track")
+    core, chip = lax.rem(track, 2), lax.div(track, 2)
+    partner = track_place(chip * 2 + 1 - core)
+    own_rows = pl.ds(pl.multiple_of(core * half, 8), half)
+    other_rows = pl.ds(pl.multiple_of((1 - core) * half, 8), half)
+
+    def ahead(step):
+        q = lax.rem(chip + step, chips)
+        return q, track_place(q * 2 + core), pl.ds(pl.multiple_of(q * width, 128), width)
+
+    def copy(source, target, phase, sent, landed, device):
+        return pltpu.make_async_remote_copy(
+            src_ref=source, dst_ref=target, send_sem=send.at[phase, sent],
+            recv_sem=recv.at[phase, landed], device_id=device,
+            device_id_type=pl.DeviceIdType.MESH,
+        )
+
+    barrier = pltpu.get_barrier_semaphore()
+    pl.semaphore_signal(barrier, inc=1, device_id=partner, device_id_type=pl.DeviceIdType.MESH)
+    for step in range(1, chips):
+        pl.semaphore_signal(
+            barrier, inc=1, device_id=ahead(step)[1], device_id_type=pl.DeviceIdType.MESH
+        )
+    pl.semaphore_wait(barrier, chips)
+
+    started = []
+    for step in range(1, chips + 1):
+        q, _, lanes = ahead(step)
+        pair = copy(x_ref.at[:, other_rows, lanes], paired.at[q], 0, q, q, partner)
+        pair.start()
+        started.append(pair)
+    for step in range(1, chips + 1):
+        q, peer, lanes = ahead(step)
+        started[step - 1].wait_recv()
+        mine[q] = x_ref[:, own_rows, lanes] + paired[q]
+        if step < chips:
+            scatter = copy(mine.at[q], slots.at[chip], 1, q, chip, peer)
+            scatter.start()
+            started.append(scatter)
+    total = mine[chip]
+    for step in range(1, chips):
+        q, peer, _ = ahead(chips - step)
+        copy(mine.at[q], slots.at[q], 1, q, q, peer).wait_recv()
+        total = total + slots[q]
+    gathered[chip] = total
+    for step in range(1, chips):
+        q, peer, _ = ahead(step)
+        gather = copy(gathered.at[chip], gathered.at[chip], 2, q, chip, peer)
+        gather.start()
+        started.append(gather)
+    forward = copy(gathered.at[chip], other.at[chip], 3, chip, chip, partner)
+    forward.start()
+    started.append(forward)
+    for step in range(1, chips):
+        q, peer, _ = ahead(chips - step)
+        copy(gathered.at[q], gathered.at[q], 2, q, q, peer).wait_recv()
+        forward = copy(gathered.at[q], other.at[q], 3, q, q, partner)
+        forward.start()
+        started.append(forward)
+    for q in range(chips):
+        out_ref[:, own_rows, q * width:(q + 1) * width] = gathered[q]
+    for q in range(chips):
+        copy(other.at[q], other.at[q], 3, q, q, partner).wait_recv()
+        out_ref[:, other_rows, q * width:(q + 1) * width] = other[q]
+    for item in started:
+        item.wait_send()
+
+
+def stats_total(sums, tracks):
+    chips = tracks // 2
+    _, bands, lanes = sums.shape
+    piece = (chips, 2, bands // 2, lanes // chips)
+    return pl.pallas_call(
+        functools.partial(stats_kernel, tracks),
+        out_shape=jax.ShapeDtypeStruct(sums.shape, jnp.float32),
+        in_specs=[pl.BlockSpec(memory_space=pltpu.VMEM)],
+        out_specs=pl.BlockSpec(memory_space=pltpu.VMEM),
+        scratch_shapes=[pltpu.VMEM(piece, jnp.float32)] * 5
+        + [pltpu.SemaphoreType.DMA((4, chips))] * 2,
+        compiler_params=pltpu.CompilerParams(collective_id=1, has_side_effects=True),
+        name="stats_total",
+    )(sums)
+
+
+def gram_kernel(lines, tracks, x_ref, out_ref, slots, full, send, recv):
+    count = lines * tracks
+    me = lax.axis_index("line") * tracks + lax.axis_index("track")
+
+    def ahead(step):
+        peer = lax.rem(me + step, count)
+        return peer, (lax.div(peer, tracks), lax.rem(peer, tracks))
+
+    def settle(ref, sem):
+        everyone = ref.at[pl.ds(0, count - 1)]
+        pltpu.make_async_copy(everyone, everyone, sem).wait()
+
+    barrier = pltpu.get_barrier_semaphore()
+
+    @pl.loop(1, count)
+    def _(step):
+        pl.semaphore_signal(
+            barrier, inc=1, device_id=ahead(step)[1], device_id_type=pl.DeviceIdType.MESH
+        )
+
+    pl.semaphore_wait(barrier, count - 1)
+
+    @pl.loop(1, count)
+    def _(step):
+        peer, place = ahead(step)
+        pltpu.make_async_remote_copy(
+            src_ref=x_ref.at[peer], dst_ref=slots.at[me], send_sem=send.at[0],
+            recv_sem=recv.at[0], device_id=place, device_id_type=pl.DeviceIdType.MESH,
+        ).start()
+
+    slots[me] = x_ref[me]
+    settle(slots, recv.at[0])
+    full[me] = jnp.sum(slots[...], axis=0)
+
+    @pl.loop(1, count)
+    def _(step):
+        pltpu.make_async_remote_copy(
+            src_ref=full.at[me], dst_ref=full.at[me], send_sem=send.at[1],
+            recv_sem=recv.at[1], device_id=ahead(step)[1],
+            device_id_type=pl.DeviceIdType.MESH,
+        ).start()
+
+    settle(full, recv.at[1])
+    out_ref[...] = full[...]
+    settle(x_ref, send.at[0])
+    settle(full, send.at[1])
+
+
+def gram_total(packed, lines, tracks):
+    count = lines * tracks
+    height, wide = packed.shape
+    rows = -(-height // (8 * count)) * 8
+    padded = jnp.pad(packed, ((0, count * rows - height), (0, 0)))
+    piece = (count, rows, wide)
+    total = pl.pallas_call(
+        functools.partial(gram_kernel, lines, tracks),
+        out_shape=jax.ShapeDtypeStruct(piece, jnp.float32),
+        in_specs=[pl.BlockSpec(memory_space=pltpu.VMEM)],
+        out_specs=pl.BlockSpec(memory_space=pltpu.VMEM),
+        scratch_shapes=[pltpu.VMEM(piece, jnp.float32)] * 2
+        + [pltpu.SemaphoreType.DMA((2,))] * 2,
+        compiler_params=pltpu.CompilerParams(collective_id=0, has_side_effects=True),
+        name="gram_total",
+    )(padded.reshape(piece))
+    return total.reshape(count * rows, wide)[:height]
+
+
+def pack_grams(signal_part, noise_part, wide):
+    size = signal_part.shape[0]
+    above = jnp.arange(size)[:, None] < jnp.arange(size)[None, :]
+    square = jnp.where(above, signal_part, noise_part)
+    packed = jnp.concatenate([square, jnp.diagonal(signal_part)[None]], axis=0)
+    return jnp.pad(packed, ((0, wide - size - 1), (0, wide - size)))
 
 
 def body(radiance):
@@ -131,9 +300,11 @@
     line_count = lax.axis_size("line")
     total_rows = row_count * track_count
     values = local_block.astype(jnp.float32)
-    first_sum = jnp.sum(values, axis=0)
-    second_sum = jnp.sum(values * values, axis=0)
-    first_total, second_total = lax.psum((first_sum, second_sum), "track")
+    sums = jnp.stack([jnp.sum(values, axis=0), jnp.sum(values * values, axis=0)])
+    strip = 128 * (track_count // 2)
+    margin = -column_count % strip
+    totals = stats_total(jnp.pad(sums, ((0, 0), (0, 0), (0, margin))), track_count)
+    first_total, second_total = totals[0, :, :column_count], totals[1, :, :column_count]
     col_mean, factor, band_mean = column_terms(first_total, second_total, total_rows)
     centred = ((values - col_mean) * factor).astype(jnp.bfloat16)
     following = from_behind(centred[:1], "track", -1)
@@ -148,10 +319,12 @@
     noise_part = jnp.einsum(
         "rbc,rdc->bd", differences, differences, preferred_element_type=jnp.float32
     )
-    signal_total, noise_total = lax.psum((signal_part, noise_part), ("line", "track"))
+    size = signal_part.shape[0]
+    wide = (size // 128 + 1) * 128
+    packed = gram_total(pack_grams(signal_part, noise_part, wide), line_count, track_count)
     signal_count = line_count * total_rows * column_count
     noise_count = 2 * line_count * (total_rows - 1) * column_count
-    filter_matrix = mnf_filter(signal_total, noise_total, signal_count, noise_count, NCOMP)
+    filter_matrix = mnf_filter(packed, size, signal_count, noise_count, NCOMP)
     narrow = filter_matrix.astype(jnp.bfloat16)
     mixed = jnp.einsum("ab,rac->rbc", narrow, centred, preferred_element_type=jnp.float32)
     cleaned = (band_mean[:, None] + mixed).astype(jnp.bfloat16)

time: 282 us -> 119 us (0.42)
  waiting for transfers between devices: 234 us -> 0.01 us
  Pallas kernels: 16.8 us -> 96.9 us
  between operations: 14.1 us -> 0.79 us
  local copies, waits for them, and re-layouts: 1.18 us -> 6.17 us
    psum x2 -> x0, waiting for transfers between devices: 233 us -> none  [the longest x1 132 us: body(): lax.psum((signal_part, noise_part), ('line', 'track'))]
    pallas_call x1 -> x3, Pallas kernels: 16.8 us -> 96.9 us  [the longest x1 46.2 us: stats_total(): pl.pallas_call(functools.partial(stats_kernel, tracks), out_shape=jax.Sha...]
  transfers between devices with their start and end apart: 3 -> 1, of which waited for: 3 -> 0; matrix products, arithmetic and copies ran while one was open for 1% -> 3% of each run, Pallas kernels for 0% -> 0%
where the time goes in v2:
time: 119 us; the launch traced here: 118 us
  Pallas kernels  96.9 us (81%)
  other arithmetic  7.02 us (6%)
  matrix products  6.19 us (5%)
  local copies, waits for them, and re-layouts  6.17 us (5%)
  starting transfers between devices  1.28 us (1%)
    pallas_call x1, Pallas kernels, stats_total(): pl.pallas_call(functools.partial(stats_kernel, tracks), out_shape=jax.Sha...  46.2 us
    pallas_call x1, Pallas kernels, gram_total(): pl.pallas_call(functools.partial(gram_kernel, lines, tracks), out_shape=j...  34 us
    pallas_call x1, Pallas kernels, mnf_filter(): pl.pallas_call(functools.partial(mnf_kernel, 1.0 / signal_count, 1.0 / no...  16.7 us
    dot_general x1, matrix products, body(): jnp.einsum('ab,rac->rbc', narrow, centred, preferred_element_type=jnp.flo...  3.01 us
    dot_general x1, matrix products, body(): jnp.einsum('rbc,rdc->bd', differences, differences, preferred_element_typ...  2.51 us
  transfers between devices with their start and end apart: 1, of which 0 were waited for; matrix products, arithmetic and copies ran while one was open for 3% of the time, Pallas kernels for 0%

profile of v2, /device:TPU:0, one launch (start us, length us, event | category | flops | bytes accessed | tf_op | source)
XLA Modules:
  0.0 118.4 jit_solution(2118787705054300936)
XLA Ops:
  0.6 0.0 copy-start.1
  0.6 2.1 %fusion.2 = f32[224,1000]{1,0:T(8,128)S(1)} fusion(bf16[1,4,224,1000]{3,2,1,0:T(8,128)(2,1)} %param.1), kind=kLoop, calls=%fused_computation.5 | loop fusion | flops 2464000 | bytes 2688000 | tf_op jit(solution)/shard_map/reduce_sum | solution.py:303
  2.8 0.0 copy-done.1
  2.8 0.3 convert_reduce_fusion
  3.1 1.4 %select_maximum_fusion.x_ref = f32[2,224,1024]{2,1,0:T(8,128)} fusion(f32[1,224,1000]{2,1,0:T(8,128)S(1)} %bitcast.40, f32[1,224,1000]{2,1,0:T(8,128)S(1)} %bitcast.41), kind=kLoop, calls=%fused_computation.11 | loop fusion | flops 1835008 | bytes 3627008 | tf_op jit(solution)/shard_map/stack | solution.py:303
  4.5 46.2 %stats_total.1 = f32[2,224,1024]{2,1,0:T(8,128)} custom-call(f32[2,224,1024]{2,1,0:T(8,128)} %select_maximum_fusion.x_ref), custom_call_target="tpu_custom_call" | custom-call | tf_op jit(solution)/shard_map/stats_total/pallas_call | solution.py:208
  50.7 0.0 copy-start
  50.7 2.2 %fusion.14 = (f32[224]{0:T(256)S(1)}, f32[224]{0:T(256)S(1)}) fusion(f32[2,224,1024]{2,1,0:T(8,128)} %stats_total.1), kind=kLoop, calls=%fused_computation.26 | loop fusion | flops 1567552 | bytes 1793792 | tf_op jit(solution)/shard_map/reduce_sum | solution.py:27
  53.0 0.0 copy-done
  53.0 0.0 copy-start.2
  53.0 0.2 fusion.13
  53.2 1.3 %copy-done.2 = bf16[1,4,224,1000]{3,2,1,0:T(8,128)(2,1)S(1)} copy-done((bf16[1,4,224,1000]{3,2,1,0:T(8,128)(2,1)S(1)}, bf16[1,4,224,1000]{3,2,1,0:T(8,128)(2,1)}, u32[]{:S(2)}) %copy-start.2) | copy-done | bytes 1792024
  54.5 0.6 fusion.4
  55.1 0.8 slice.19
  55.9 1.3 %collective-permute-start = (bf16[1,224,1000]{2,1,0:T(8,128)(2,1)}, bf16[1,224,1000]{2,1,0:T(8,128)(2,1)}, u32[]{:S(2)}, u32[]{:S(2)}) collective-permute-start(bf16[1,224,1000]{2,1,0:T(8,128)(2,1)} %slice.19), channel_id=1, source_target_pairs={{1,0},{2,1},{3,2},{4,3},{5,4},{6,5},{7,6},{8,7},{9,8},{10,9},{11,1... | collective-permute-start | bytes 1344008 | tf_op jit(solution)/shard_map/ppermute | solution.py:21
  57.2 0.1 slice.18
  57.3 0.7 convolution_bitcast_fusion
  58.0 2.4 %gather_fusion = f32[224]{0:T(256)S(1)} fusion(f32[224,224]{0,1:T(8,128)S(1)} %convolution_bitcast_fusion, s32[224]{0:T(256)S(1)} %bitcast.39), kind=kCustom, calls=%fused_computation | custom fusion | bytes 3584 | tf_op jit(solution)/shard_map/jit(diagonal)/cond/branch_0_fun/gather | solution.py:291
  60.3 0.8 copy.5
  61.1 0.0 copy-start.3
  61.1 0.0 collective-permute-done
  61.1 2.5 %fusion.12 = f32[224,224]{0,1:T(8,128)S(1)} fusion(f32[224,224]{0,1:T(8,128)S(1)} %convolution_bitcast_fusion, bf16[4,224,1000]{2,1,0:T(8,128)(2,1)S(1)} %fusion.4, bf16[1,224,1000]{2,1,0:T(8,128)(2,1)} %collective-permute-done, bf16[3,224,1000]{2,1,0:T(8,128)(2,1)S(1)} %slice.18, f32[4]{0:T(128)S(1)} %or_select_fusion), kind=kOutput, calls=%fused_computation.20 | convolution fusion | flops 406884352 | bytes 3985424 | tf_op jit(solution)/shard_map/rbc,rdc->bd/dot_general | solution.py:319
  63.6 0.0 copy-done.3
  63.7 0.1 pad_maximum_fusion
  63.8 0.1 copy.10
  63.9 0.7 pad_bitcast_fusion.x_ref
  64.6 34.0 %gram_total.1 = f32[32,8,256]{2,1,0:T(8,128)} custom-call(f32[32,8,256]{2,1,0:T(8,128)} %pad_bitcast_fusion.x_ref), custom_call_target="tpu_custom_call" | custom-call | tf_op jit(solution)/shard_map/gram_total/pallas_call | solution.py:274
  98.6 16.7 %mnf_filter.1 = f32[224,224]{1,0:T(8,128)} custom-call(f32[256,256]{1,0:T(8,128)} %bitcast.42), custom_call_target="tpu_custom_call" | custom-call | tf_op jit(solution)/shard_map/mnf_filter/pallas_call | solution.py:118
  115.4 3.0 %fusion.10 = bf16[1,4,224,1000]{3,2,1,0:T(8,128)(2,1)} fusion(bf16[4,224,1000]{2,1,0:T(8,128)(2,1)S(1)} %fusion.4, f32[224]{0:T(256)S(1)} %get-tuple-element.7, f32[224,224]{1,0:T(8,128)} %mnf_filter.1), kind=kOutput, calls=%fused_computation.17 | convolution fusion | flops 403250176 | bytes 3785600 | tf_op jit(solution)/shard_map/ab,rac->rbc/dot_general | solution.py:329
  (3 shorter events, 0.0 us)
Async XLA Ops:
  0.6 2.2 %copy-start.1 = (bf16[1,4,224,1000]{3,2,1,0:T(8,128)(2,1)S(1)}, bf16[1,4,224,1000]{3,2,1,0:T(8,128)(2,1)}, u32[]{:S(2)}) copy-start(bf16[1,4,224,1000]{3,2,1,0:T(8,128)(2,1)} %param.1) | copy-start | bytes 5376004
  50.7 2.3 %copy-start = (f32[2,224,1024]{2,1,0:T(8,128)S(1)}, f32[2,224,1024]{2,1,0:T(8,128)}, u32[]{:S(2)}) copy-start(f32[2,224,1024]{2,1,0:T(8,128)} %stats_total.1) | copy-start | bytes 5505028
  53.0 1.5 %copy-start.2 = (bf16[1,4,224,1000]{3,2,1,0:T(8,128)(2,1)S(1)}, bf16[1,4,224,1000]{3,2,1,0:T(8,128)(2,1)}, u32[]{:S(2)}) copy-start(bf16[1,4,224,1000]{3,2,1,0:T(8,128)(2,1)} %param.1) | copy-start | bytes 5376004
  55.9 5.3 %collective-permute-start = (bf16[1,224,1000]{2,1,0:T(8,128)(2,1)}, bf16[1,224,1000]{2,1,0:T(8,128)(2,1)}, u32[]{:S(2)}, u32[]{:S(2)}) collective-permute-start(bf16[1,224,1000]{2,1,0:T(8,128)(2,1)} %slice.19), channel_id=1, source_target_pairs={{1,0},{2,1},{3,2},{4,3},{5,4},{6,5},{7,6},{8,7},{9,8},{10,9},{11,1... | collective-permute-start | bytes 1344008 | tf_op jit(solution)/shard_map/ppermute | solution.py:21
  61.1 2.5 %copy-start.3 = (f32[1,224]{0,1:T(8,128)S(1)}, f32[1,224]{0,1:T(8,128)}, u32[]{:S(2)}) copy-start(f32[1,224]{0,1:T(8,128)} %copy.5) | copy-start | bytes 2692

commit v3 on v2

--- a/solution.py
+++ b/solution.py
@@ -217,70 +217,89 @@
     )(sums)
 
 
-def gram_kernel(lines, tracks, x_ref, out_ref, slots, full, send, recv):
-    count = lines * tracks
-    me = lax.axis_index("line") * tracks + lax.axis_index("track")
-
-    def ahead(step):
-        peer = lax.rem(me + step, count)
-        return peer, (lax.div(peer, tracks), lax.rem(peer, tracks))
-
-    def settle(ref, sem):
-        everyone = ref.at[pl.ds(0, count - 1)]
-        pltpu.make_async_copy(everyone, everyone, sem).wait()
+def gram_kernel(lines, chips, x_ref, out_ref, paired, by_line, by_chip, half, quarter, full, send, recv):
+    line = lax.axis_index("line")
+    track = lax.axis_index("track")
+    core, chip = lax.rem(track, 2), lax.div(track, 2)
+    partner = (line, chip * 2 + 1 - core)
+    other_lines = [(q, (q, track)) for q in (lax.rem(line + s, lines) for s in range(1, lines))]
+    other_chips = [
+        (q, (line, q * 2 + core)) for q in (lax.rem(chip + s, chips) for s in range(1, chips))
+    ]
+    started = []
+
+    def copy(source, target, phase, sent, landed, device):
+        return pltpu.make_async_remote_copy(
+            src_ref=source, dst_ref=target, send_sem=send.at[phase, sent],
+            recv_sem=recv.at[phase, landed], device_id=device,
+            device_id_type=pl.DeviceIdType.MESH,
+        )
+
+    def launch(*args):
+        item = copy(*args)
+        item.start()
+        started.append(item)
 
     barrier = pltpu.get_barrier_semaphore()
-
-    @pl.loop(1, count)
-    def _(step):
-        pl.semaphore_signal(
-            barrier, inc=1, device_id=ahead(step)[1], device_id_type=pl.DeviceIdType.MESH
-        )
-
-    pl.semaphore_wait(barrier, count - 1)
-
-    @pl.loop(1, count)
-    def _(step):
-        peer, place = ahead(step)
-        pltpu.make_async_remote_copy(
-            src_ref=x_ref.at[peer], dst_ref=slots.at[me], send_sem=send.at[0],
-            recv_sem=recv.at[0], device_id=place, device_id_type=pl.DeviceIdType.MESH,
-        ).start()
-
-    slots[me] = x_ref[me]
-    settle(slots, recv.at[0])
-    full[me] = jnp.sum(slots[...], axis=0)
-
-    @pl.loop(1, count)
-    def _(step):
-        pltpu.make_async_remote_copy(
-            src_ref=full.at[me], dst_ref=full.at[me], send_sem=send.at[1],
-            recv_sem=recv.at[1], device_id=ahead(step)[1],
-            device_id_type=pl.DeviceIdType.MESH,
-        ).start()
-
-    settle(full, recv.at[1])
+    for place in [partner] + [place for _, place in other_lines + other_chips]:
+        pl.semaphore_signal(barrier, inc=1, device_id=place, device_id_type=pl.DeviceIdType.MESH)
+    pl.semaphore_wait(barrier, lines + chips - 1)
+
+    launch(x_ref.at[1 - core], paired, 0, 0, 0, partner)
+    copy(paired, paired, 0, 0, 0, partner).wait_recv()
+    half[...] = x_ref[core] + paired[...]
+    for q, place in other_lines:
+        launch(half.at[q], by_line.at[line], 1, q, line, place)
+    part = half[line]
+    for q, place in other_lines:
+        copy(by_line.at[q], by_line.at[q], 1, q, q, place).wait_recv()
+        part = part + by_line[q]
+    quarter[...] = part
+    for q, place in other_chips:
+        launch(quarter.at[q], by_chip.at[chip], 2, q, chip, place)
+    total = quarter[chip]
+    for q, place in other_chips[::-1]:
+        copy(by_chip.at[q], by_chip.at[q], 2, q, q, place).wait_recv()
+        total = total + by_chip[q]
+    full[core, line, chip] = total
+    own = full.at[core, line, chip]
+    for q, place in other_chips:
+        launch(own, own, 3, q, chip, place)
+    for q, place in other_chips[::-1]:
+        copy(full.at[core, line, q], full.at[core, line, q], 3, q, q, place).wait_recv()
+    own = full.at[core, line]
+    for q, place in other_lines:
+        launch(own, own, 4, q, line, place)
+    for q, place in other_lines:
+        copy(full.at[core, q], full.at[core, q], 4, q, q, place).wait_recv()
+    own = full.at[core]
+    launch(own, own, 5, 0, 0, partner)
+    copy(full.at[1 - core], full.at[1 - core], 5, 0, 0, partner).wait_recv()
     out_ref[...] = full[...]
-    settle(x_ref, send.at[0])
-    settle(full, send.at[1])
+    for item in started:
+        item.wait_send()
 
 
 def gram_total(packed, lines, tracks):
+    chips = tracks // 2
     count = lines * tracks
     height, wide = packed.shape
     rows = -(-height // (8 * count)) * 8
     padded = jnp.pad(packed, ((0, count * rows - height), (0, 0)))
-    piece = (count, rows, wide)
+    piece = (rows, wide)
+    whole = (2, lines, chips) + piece
+    shapes = [(lines, chips) + piece, (lines, chips) + piece, (chips,) + piece,
+              (lines, chips) + piece, (chips,) + piece, whole]
     total = pl.pallas_call(
-        functools.partial(gram_kernel, lines, tracks),
-        out_shape=jax.ShapeDtypeStruct(piece, jnp.float32),
+        functools.partial(gram_kernel, lines, chips),
+        out_shape=jax.ShapeDtypeStruct(whole, jnp.float32),
         in_specs=[pl.BlockSpec(memory_space=pltpu.VMEM)],
         out_specs=pl.BlockSpec(memory_space=pltpu.VMEM),
-        scratch_shapes=[pltpu.VMEM(piece, jnp.float32)] * 2
-        + [pltpu.SemaphoreType.DMA((2,))] * 2,
+        scratch_shapes=[pltpu.VMEM(shape, jnp.float32) for shape in shapes]
+        + [pltpu.SemaphoreType.DMA((6, max(lines, chips)))] * 2,
         compiler_params=pltpu.CompilerParams(collective_id=0, has_side_effects=True),
         name="gram_total",
-    )(padded.reshape(piece))
+    )(padded.reshape(whole))
     return total.reshape(count * rows, wide)[:height]
 
 

time: 119 us -> 121 us (1.017)
  Pallas kernels: 96.9 us -> 99 us
    pallas_call x1, Pallas kernels: 34 us -> 36.1 us  [gram_total(): pl.pallas_call(functools.partial(gram_kernel, lines, chips), out_shape=ja...]
where the time goes in v3:
time: 121 us
  Pallas kernels  99 us (82%)
  other arithmetic  7.02 us (6%)
  local copies, waits for them, and re-layouts  6.36 us (5%)
  matrix products  6.19 us (5%)
  starting transfers between devices  1.28 us (1%)
    pallas_call x1, Pallas kernels, stats_total(): pl.pallas_call(functools.partial(stats_kernel, tracks), out_shape=jax.Sha...  46.2 us
    pallas_call x1, Pallas kernels, gram_total(): pl.pallas_call(functools.partial(gram_kernel, lines, chips), out_shape=ja...  36.1 us
    pallas_call x1, Pallas kernels, mnf_filter(): pl.pallas_call(functools.partial(mnf_kernel, 1.0 / signal_count, 1.0 / no...  16.7 us
    dot_general x1, matrix products, body(): jnp.einsum('ab,rac->rbc', narrow, centred, preferred_element_type=jnp.flo...  3.01 us
    gather x1, local copies, waits for them, and re-layouts, pack_grams(): packed = jnp.concatenate([square, jnp.diagonal(signal_part)[None]], axis=0)  2.55 us
    dot_general x1, matrix products, body(): jnp.einsum('rbc,rdc->bd', differences, differences, preferred_element_typ...  2.51 us
  transfers between devices with their start and end apart: 1, of which 0 were waited for; matrix products, arithmetic and copies ran while one was open for 3% of the time, Pallas kernels for 0%

profile of v3, /device:TPU:0, one launch (start us, length us, event | category | flops | bytes accessed | tf_op | source)
XLA Modules:
  0.0 120.6 jit_solution(1418767685357820051)
XLA Ops:
  0.6 0.0 copy-start.1
  0.6 2.1 %fusion.2 = f32[224,1000]{1,0:T(8,128)S(1)} fusion(bf16[1,4,224,1000]{3,2,1,0:T(8,128)(2,1)} %param.1), kind=kLoop, calls=%fused_computation.5 | loop fusion | flops 2464000 | bytes 2688000 | tf_op jit(solution)/shard_map/reduce_sum | solution.py:322
  2.8 0.0 copy-done.1
  2.8 0.3 convert_reduce_fusion
  3.1 1.4 %select_maximum_fusion.x_ref = f32[2,224,1024]{2,1,0:T(8,128)} fusion(f32[1,224,1000]{2,1,0:T(8,128)S(1)} %bitcast.39, f32[1,224,1000]{2,1,0:T(8,128)S(1)} %bitcast.40), kind=kLoop, calls=%fused_computation.11 | loop fusion | flops 1835008 | bytes 3627008 | tf_op jit(solution)/shard_map/stack | solution.py:322
  4.5 46.2 %stats_total.1 = f32[2,224,1024]{2,1,0:T(8,128)} custom-call(f32[2,224,1024]{2,1,0:T(8,128)} %select_maximum_fusion.x_ref), custom_call_target="tpu_custom_call" | custom-call | tf_op jit(solution)/shard_map/stats_total/pallas_call | solution.py:208
  50.7 0.0 copy-start
  50.7 2.2 %fusion.14 = (f32[224]{0:T(256)S(1)}, f32[224]{0:T(256)S(1)}) fusion(f32[2,224,1024]{2,1,0:T(8,128)} %stats_total.1), kind=kLoop, calls=%fused_computation.26 | loop fusion | flops 1567552 | bytes 1793792 | tf_op jit(solution)/shard_map/reduce_sum | solution.py:27
  53.0 0.0 copy-done
  53.0 0.0 copy-start.2
  53.0 0.2 fusion.13
  53.2 1.3 %copy-done.2 = bf16[1,4,224,1000]{3,2,1,0:T(8,128)(2,1)S(1)} copy-done((bf16[1,4,224,1000]{3,2,1,0:T(8,128)(2,1)S(1)}, bf16[1,4,224,1000]{3,2,1,0:T(8,128)(2,1)}, u32[]{:S(2)}) %copy-start.2) | copy-done | bytes 1792024
  54.5 0.6 fusion.4
  55.1 0.8 slice.19
  55.9 1.3 %collective-permute-start = (bf16[1,224,1000]{2,1,0:T(8,128)(2,1)}, bf16[1,224,1000]{2,1,0:T(8,128)(2,1)}, u32[]{:S(2)}, u32[]{:S(2)}) collective-permute-start(bf16[1,224,1000]{2,1,0:T(8,128)(2,1)} %slice.19), channel_id=1, source_target_pairs={{1,0},{2,1},{3,2},{4,3},{5,4},{6,5},{7,6},{8,7},{9,8},{10,9},{11,1... | collective-permute-start | bytes 1344008 | tf_op jit(solution)/shard_map/ppermute | solution.py:21
  57.2 0.1 slice.18
  57.3 0.7 convolution_bitcast_fusion
  58.0 2.5 %gather_fusion = f32[224]{0:T(256)S(1)} fusion(f32[224,224]{0,1:T(8,128)S(1)} %convolution_bitcast_fusion, s32[224]{0:T(256)S(1)} %bitcast.38), kind=kCustom, calls=%fused_computation | custom fusion | bytes 3584 | tf_op jit(solution)/shard_map/jit(diagonal)/cond/branch_0_fun/gather | solution.py:310
  60.5 0.8 copy.5
  61.3 0.0 copy-start.3
  61.3 0.0 collective-permute-done
  61.3 2.5 %fusion.12 = f32[224,224]{0,1:T(8,128)S(1)} fusion(f32[224,224]{0,1:T(8,128)S(1)} %convolution_bitcast_fusion, bf16[4,224,1000]{2,1,0:T(8,128)(2,1)S(1)} %fusion.4, bf16[1,224,1000]{2,1,0:T(8,128)(2,1)} %collective-permute-done, bf16[3,224,1000]{2,1,0:T(8,128)(2,1)S(1)} %slice.18, f32[4]{0:T(128)S(1)} %or_select_fusion), kind=kOutput, calls=%fused_computation.20 | convolution fusion | flops 406884352 | bytes 3985424 | tf_op jit(solution)/shard_map/rbc,rdc->bd/dot_general | solution.py:338
  63.8 0.0 copy-done.3
  63.8 0.1 pad_maximum_fusion
  63.9 0.1 copy.10
  64.1 0.7 pad.9.clone
  64.8 36.1 %gram_total.1 = f32[2,2,8,8,256]{4,3,2,1,0:T(8,128)} custom-call(f32[2,2,8,8,256]{4,3,2,1,0:T(8,128)} %bitcast.41), custom_call_target="tpu_custom_call" | custom-call | tf_op jit(solution)/shard_map/gram_total/pallas_call | solution.py:293
  100.9 16.7 %mnf_filter.1 = f32[224,224]{1,0:T(8,128)} custom-call(f32[256,256]{1,0:T(8,128)} %bitcast.42), custom_call_target="tpu_custom_call" | custom-call | tf_op jit(solution)/shard_map/mnf_filter/pallas_call | solution.py:118
  117.6 3.0 %fusion.10 = bf16[1,4,224,1000]{3,2,1,0:T(8,128)(2,1)} fusion(bf16[4,224,1000]{2,1,0:T(8,128)(2,1)S(1)} %fusion.4, f32[224]{0:T(256)S(1)} %get-tuple-element.7, f32[224,224]{1,0:T(8,128)} %mnf_filter.1), kind=kOutput, calls=%fused_computation.17 | convolution fusion | flops 403250176 | bytes 3785600 | tf_op jit(solution)/shard_map/ab,rac->rbc/dot_general | solution.py:348
  (3 shorter events, 0.0 us)
Async XLA Ops:
  0.6 2.2 %copy-start.1 = (bf16[1,4,224,1000]{3,2,1,0:T(8,128)(2,1)S(1)}, bf16[1,4,224,1000]{3,2,1,0:T(8,128)(2,1)}, u32[]{:S(2)}) copy-start(bf16[1,4,224,1000]{3,2,1,0:T(8,128)(2,1)} %param.1) | copy-start | bytes 5376004
  50.7 2.3 %copy-start = (f32[2,224,1024]{2,1,0:T(8,128)S(1)}, f32[2,224,1024]{2,1,0:T(8,128)}, u32[]{:S(2)}) copy-start(f32[2,224,1024]{2,1,0:T(8,128)} %stats_total.1) | copy-start | bytes 5505028
  53.0 1.5 %copy-start.2 = (bf16[1,4,224,1000]{3,2,1,0:T(8,128)(2,1)S(1)}, bf16[1,4,224,1000]{3,2,1,0:T(8,128)(2,1)}, u32[]{:S(2)}) copy-start(bf16[1,4,224,1000]{3,2,1,0:T(8,128)(2,1)} %param.1) | copy-start | bytes 5376004
  55.9 5.4 %collective-permute-start = (bf16[1,224,1000]{2,1,0:T(8,128)(2,1)}, bf16[1,224,1000]{2,1,0:T(8,128)(2,1)}, u32[]{:S(2)}, u32[]{:S(2)}) collective-permute-start(bf16[1,224,1000]{2,1,0:T(8,128)(2,1)} %slice.19), channel_id=1, source_target_pairs={{1,0},{2,1},{3,2},{4,3},{5,4},{6,5},{7,6},{8,7},{9,8},{10,9},{11,1... | collective-permute-start | bytes 1344008 | tf_op jit(solution)/shard_map/ppermute | solution.py:21
  61.3 2.5 %copy-start.3 = (f32[1,224]{0,1:T(8,128)S(1)}, f32[1,224]{0,1:T(8,128)}, u32[]{:S(2)}) copy-start(f32[1,224]{0,1:T(8,128)} %copy.5) | copy-start | bytes 2692

commit v4 on v2

--- a/solution.py
+++ b/solution.py
@@ -288,7 +288,8 @@
     size = signal_part.shape[0]
     above = jnp.arange(size)[:, None] < jnp.arange(size)[None, :]
     square = jnp.where(above, signal_part, noise_part)
-    packed = jnp.concatenate([square, jnp.diagonal(signal_part)[None]], axis=0)
+    diagonal = jnp.sum(jnp.where(jnp.eye(size, dtype=bool), signal_part, 0.0), axis=0)
+    packed = jnp.concatenate([square, diagonal[None]], axis=0)
     return jnp.pad(packed, ((0, wide - size - 1), (0, wide - size)))
 
 
@@ -299,6 +300,7 @@
     track_count = lax.axis_size("track")
     line_count = lax.axis_size("line")
     total_rows = row_count * track_count
+    ahead = from_behind(local_block[:1], "track", -1)
     values = local_block.astype(jnp.float32)
     sums = jnp.stack([jnp.sum(values, axis=0), jnp.sum(values * values, axis=0)])
     strip = 128 * (track_count // 2)
@@ -307,7 +309,7 @@
     first_total, second_total = totals[0, :, :column_count], totals[1, :, :column_count]
     col_mean, factor, band_mean = column_terms(first_total, second_total, total_rows)
     centred = ((values - col_mean) * factor).astype(jnp.bfloat16)
-    following = from_behind(centred[:1], "track", -1)
+    following = ((ahead.astype(jnp.float32) - col_mean) * factor).astype(jnp.bfloat16)
     rows_ahead = jnp.concatenate([centred[1:], following], axis=0)
     keep_last = lax.axis_index("track") < track_count - 1
     row_index = jnp.arange(row_count)

time: 119 us -> 115 us (0.966)
  local copies, waits for them, and re-layouts: 6.17 us -> 2.72 us
  Pallas kernels: 96.9 us -> 93.9 us
  other arithmetic: 7.02 us -> 8.35 us
    pallas_call x1, Pallas kernels: 34 us -> 30.1 us  [gram_total(): pl.pallas_call(functools.partial(gram_kernel, lines, tracks), out_shape=j...]
    gather x1 -> x0, local copies, waits for them, and re-layouts: 2.37 us -> none  [pack_grams(): packed = jnp.concatenate([square, jnp.diagonal(signal_part)[None]], axis=0)]
    convert_element_type x0 -> x1, other arithmetic: none -> 1.82 us  [body(): ((ahead.astype(jnp.float32) - col_mean) * factor).astype(jnp.bfloat16)]
    reduce_sum x1, other arithmetic: 2.14 us -> 0.39 us  [body(): jnp.sum(values * values, axis=0)]
    reduce_sum x1, other arithmetic: 0.33 us -> 1.97 us  [body(): jnp.sum(values, axis=0)]
  transfers between devices with their start and end apart: 1 -> 1, of which waited for: 0 -> 0; matrix products, arithmetic and copies ran while one was open for 3% -> 5% of each run, Pallas kernels for 0% -> 41%
where the time goes in v4:
time: 115 us; the launch traced here: 114 us
  Pallas kernels  93.9 us (82%)
  other arithmetic  8.35 us (7%)
  matrix products  7.16 us (6%)
  local copies, waits for them, and re-layouts  2.72 us (2%)
  starting transfers between devices  1.29 us (1%)
    pallas_call x1, Pallas kernels, stats_total(): pl.pallas_call(functools.partial(stats_kernel, tracks), out_shape=jax.Sha...  47 us
    pallas_call x1, Pallas kernels, gram_total(): pl.pallas_call(functools.partial(gram_kernel, lines, tracks), out_shape=j...  30.1 us
    pallas_call x1, Pallas kernels, mnf_filter(): pl.pallas_call(functools.partial(mnf_kernel, 1.0 / signal_count, 1.0 / no...  16.7 us
    dot_general x1, matrix products, body(): jnp.einsum('rbc,rdc->bd', differences, differences, preferred_element_typ...  3.4 us
    dot_general x1, matrix products, body(): jnp.einsum('ab,rac->rbc', narrow, centred, preferred_element_type=jnp.flo...  3.01 us
  transfers between devices with their start and end apart: 1, of which 0 were waited for; matrix products, arithmetic and copies ran while one was open for 5% of the time, Pallas kernels for 41%

profile of v4, /device:TPU:0, one launch (start us, length us, event | category | flops | bytes accessed | tf_op | source)
XLA Modules:
  0.0 114.2 jit_solution(1688661605312398245)
XLA Ops:
  0.6 0.0 copy-start
  0.6 1.2 %slice_bitcast_fusion = bf16[1,224,1000]{2,1,0:T(8,128)(2,1)S(1)} fusion(bf16[1,4,224,1000]{3,2,1,0:T(8,128)(2,1)} %param.1), kind=kLoop, calls=%fused_computation.28 | loop fusion | bytes 896000 | tf_op jit(solution)/shard_map/slice | solution.py:303
  1.8 1.3 %collective-permute-start = (bf16[1,224,1000]{2,1,0:T(8,128)(2,1)S(1)}, bf16[1,224,1000]{2,1,0:T(8,128)(2,1)S(1)}, u32[]{:S(2)}, u32[]{:S(2)}) collective-permute-start(bf16[1,224,1000]{2,1,0:T(8,128)(2,1)S(1)} %slice_bitcast_fusion), channel_id=1, source_target_pairs={{1,0},{2,1},{3,2},{4,3},{5,4},{6,5},{7,6},{8,7},{9,8},{10,9},{11,1... | collective-permute-start | bytes 1344008 | tf_op jit(solution)/shard_map/ppermute | solution.py:21
  3.1 2.0 %convert_reduce_fusion = f32[224,1000]{1,0:T(8,128)S(1)} fusion(bf16[1,4,224,1000]{3,2,1,0:T(8,128)(2,1)} %param.1), kind=kLoop, calls=%fused_computation.1 | loop fusion | flops 1568000 | bytes 2688000 | tf_op jit(solution)/shard_map/reduce_sum | solution.py:305
  5.1 0.0 copy-done
  5.1 0.4 fusion.2
  5.5 1.4 %select_maximum_fusion.x_ref = f32[2,224,1024]{2,1,0:T(8,128)} fusion(f32[1,224,1000]{2,1,0:T(8,128)S(1)} %bitcast.41, f32[1,224,1000]{2,1,0:T(8,128)S(1)} %bitcast.40), kind=kLoop, calls=%fused_computation.10 | loop fusion | flops 1835008 | bytes 3627008 | tf_op jit(solution)/shard_map/stack | solution.py:305
  6.9 47.0 %stats_total.1 = f32[2,224,1024]{2,1,0:T(8,128)} custom-call(f32[2,224,1024]{2,1,0:T(8,128)} %select_maximum_fusion.x_ref), custom_call_target="tpu_custom_call" | custom-call | tf_op jit(solution)/shard_map/stats_total/pallas_call | solution.py:208
  53.9 2.1 %fusion.15 = (f32[224]{0:T(256)S(1)}, f32[224]{0:T(256)S(1)}) fusion(f32[2,224,1024]{2,1,0:T(8,128)} %stats_total.1), kind=kLoop, calls=%fused_computation.27 | loop fusion | flops 1567552 | bytes 1793792 | tf_op jit(solution)/shard_map/reduce_sum | solution.py:27
  56.1 0.0 collective-permute-done
  56.1 1.8 %multiply_convert_fusion.6 = (bf16[1,224,1000]{2,1,0:T(8,128)(2,1)S(1)}, f32[224,1000]{1,0:T(8,128)S(1)}, f32[224,1000]{1,0:T(8,128)S(1)}) fusion(bf16[1,224,1000]{2,1,0:T(8,128)(2,1)S(1)} %collective-permute-done, f32[2,224,1024]{2,1,0:T(8,128)} %stats_total.1, f32[224]{0:T(256)S(1)} %broadcast_multiply_fusion), kind=kLoop, calls=%fused_computation.21 | loop fusion | flops 2240000 | bytes 4480896 | tf_op jit(solution)/shard_map/convert_element_type | solution.py:312
  57.9 0.6 fusion.4
  58.5 0.0 copy-start.1
  58.5 0.8 select_reduce_fusion
  59.3 0.5 copy-done.1
  59.7 0.1 slice.20
  59.8 0.1 copy.5
  60.0 3.4 %fusion.12 = f32[224,224]{0,1:T(8,128)S(1)} fusion(f32[224,224]{0,1:T(8,128)S(1)} %get-tuple-element.8, bf16[4,224,1000]{2,1,0:T(8,128)(2,1)} %copy-done.1, bf16[1,224,1000]{2,1,0:T(8,128)(2,1)S(1)} %get-tuple-element.4, bf16[3,224,1000]{2,1,0:T(8,128)(2,1)S(1)} %slice.20, f32[4]{0:T(128)S(1)} %or_select_fusion), kind=kOutput, calls=%fused_computation.19 | convolution fusion | flops 406884352 | bytes 3985424 | tf_op jit(solution)/shard_map/rbc,rdc->bd/dot_general | solution.py:321
  63.4 0.0 copy-start.2
  63.4 0.1 pad_maximum_fusion
  63.5 0.1 copy.10
  63.6 0.7 pad_bitcast_fusion.x_ref
  64.3 30.1 %gram_total.1 = f32[32,8,256]{2,1,0:T(8,128)} custom-call(f32[32,8,256]{2,1,0:T(8,128)} %pad_bitcast_fusion.x_ref), custom_call_target="tpu_custom_call" | custom-call | tf_op jit(solution)/shard_map/gram_total/pallas_call | solution.py:274
  94.5 16.7 %mnf_filter.1 = f32[224,224]{1,0:T(8,128)} custom-call(f32[256,256]{1,0:T(8,128)} %bitcast.42), custom_call_target="tpu_custom_call" | custom-call | tf_op jit(solution)/shard_map/mnf_filter/pallas_call | solution.py:118
  111.2 0.0 copy-done.2
  111.2 3.0 %fusion.10 = bf16[1,4,224,1000]{3,2,1,0:T(8,128)(2,1)} fusion(bf16[4,224,1000]{2,1,0:T(8,128)(2,1)S(1)} %copy-done.2, f32[224]{0:T(256)S(1)} %broadcast_multiply_fusion.1, f32[224,224]{1,0:T(8,128)} %mnf_filter.1), kind=kOutput, calls=%fused_computation.16 | convolution fusion | flops 403250176 | bytes 3785600 | tf_op jit(solution)/shard_map/ab,rac->rbc/dot_general | solution.py:331
  (3 shorter events, 0.0 us)
Async XLA Ops:
  0.6 4.5 %copy-start = (bf16[1,4,224,1000]{3,2,1,0:T(8,128)(2,1)S(1)}, bf16[1,4,224,1000]{3,2,1,0:T(8,128)(2,1)}, u32[]{:S(2)}) copy-start(bf16[1,4,224,1000]{3,2,1,0:T(8,128)(2,1)} %param.1) | copy-start | bytes 5376004
  1.8 54.2 %collective-permute-start = (bf16[1,224,1000]{2,1,0:T(8,128)(2,1)S(1)}, bf16[1,224,1000]{2,1,0:T(8,128)(2,1)S(1)}, u32[]{:S(2)}, u32[]{:S(2)}) collective-permute-start(bf16[1,224,1000]{2,1,0:T(8,128)(2,1)S(1)} %slice_bitcast_fusion), channel_id=1, source_target_pairs={{1,0},{2,1},{3,2},{4,3},{5,4},{6,5},{7,6},{8,7},{9,8},{10,9},{11,1... | collective-permute-start | bytes 1344008 | tf_op jit(solution)/shard_map/ppermute | solution.py:21
  58.5 1.2 %copy-start.1 = (bf16[4,224,1000]{2,1,0:T(8,128)(2,1)}, bf16[4,224,1000]{2,1,0:T(8,128)(2,1)S(1)}, u32[]{:S(2)}) copy-start(bf16[4,224,1000]{2,1,0:T(8,128)(2,1)S(1)} %fusion.4) | copy-start | bytes 5376004
  63.4 47.9 %copy-start.2 = (bf16[4,224,1000]{2,1,0:T(8,128)(2,1)S(1)}, bf16[4,224,1000]{2,1,0:T(8,128)(2,1)}, u32[]{:S(2)}) copy-start(bf16[4,224,1000]{2,1,0:T(8,128)(2,1)} %copy-done.1) | copy-start | bytes 5376004
